TPU v7x, 32 devices: a whole 2x2x4 slice. The times are simulated.
32 devices in a mesh: gx: 16 (over z, x, core), gy: 2 (over y).
Axes of the slice: x: 2, y: 2, z: 4, core: 2. Of those that a mesh axis runs over, the one named last changes fastest.
Arguments:
- particles: float32 [64, 2, 64, 1024], P(None, None, 'gx', 'gy'), may hold values from -32 to 32, as said below
- background: float32 [2, 64, 1024], P(None, 'gx', 'gy'), may hold values from -6 to 6
- obs_tile: int32 [16, 256], P('gx', 'gy'), may hold values from 0 to 127
- obs_mask: int32 [16, 16, 256], P(None, 'gx', 'gy'), may hold values 0 or 1
- obs_value: float32 [16, 256], P('gx', 'gy'), may hold values from -6 to 6
- obs_var: float32 [16, 256], P('gx', 'gy'), may hold values from 0.1 to 1
Outputs:
- analysis: float32 [64, 2, 64, 1024], P(None, None, 'gx', 'gy')
Inputs may be any that keep to these rules, and one draw needn't show every extreme that they name: `particles`: each particle is a field of order one to a few. `obs_tile`: an observation's value names tile row t // 128 and tile column t % (128) of its slab.
All inputs are finite; a program needn't handle non-finite values. No bound on the sum of `obs_mask` on one device may be relied on, other than what follows from the above.
Results may differ from a plain program's by a relative error of at most 0.0001.
Values sent between devices are 32-bit elements; how exact they have to be, the bound alone decides.
A program may use at most 64 MiB of HBM per device.

v0:
```python
import jax
import jax.numpy as jnp
from jax import lax
from jax.sharding import PartitionSpec as P

STEPS = 2
TILE = 4
lap_weight = 0.25
prior_weight = 0.05
couple_weight = 0.5
step_length = 1.0
epsilon = 1e-06
highest = lax.Precision.HIGHEST


def with_halo(block, sides, width):
    for axis, dim in sides:
        count = lax.axis_size(axis)
        forward = [(i, i + 1) for i in range(count - 1)]
        forward.append((count - 1, 0))
        backward = [(target, source) for source, target in forward]
        low = lax.ppermute(
            lax.slice_in_dim(block, block.shape[dim] - width, None, axis=dim), axis, forward
        )
        high = lax.ppermute(lax.slice_in_dim(block, 0, width, axis=dim), axis, backward)
        block = jnp.concatenate([low, block, high], axis=dim)
    return block


def laplace_inner(field):
    total = field[..., 1:-1, 2:] + field[..., 1:-1, :-2]
    total = total + field[..., 2:, 1:-1] + field[..., :-2, 1:-1]
    return total - 4.0 * field[..., 1:-1, 1:-1]


def prior_term(deviation):
    padded = with_halo(deviation, (("gx", 2), ("gy", 3)), 2)
    smooth = padded[..., 1:-1, 1:-1] - lap_weight * laplace_inner(padded)
    curved = smooth[..., 1:-1, 1:-1] - lap_weight * laplace_inner(smooth)
    return -prior_weight * (curved + couple_weight * (deviation - deviation[:, ::-1]))


def observe_term(state, table, weights, values, variance):
    count, rows, cols = (state.shape[0], state.shape[2], state.shape[3])
    tile_rows, tile_cols = (rows // TILE, cols // TILE)
    upper = state[:, 0].reshape(count, tile_rows, TILE, tile_cols, TILE)
    cells = upper.transpose(2, 4, 0, 1, 3).reshape(TILE * TILE, count, tile_rows * tile_cols)
    picked = jnp.einsum("cpt,ot->cpo", cells, table, precision=highest)
    mapped = 0.25 * jnp.sum(weights[:, None, :] * picked, axis=0)
    innovation = (values[None, :] - mapped) / variance[None, :]
    contrib = (0.25 * weights)[:, None, :] * innovation[None]
    spread = jnp.einsum("cpo,ot->cpt", contrib, table, precision=highest)
    back = spread.reshape(TILE, TILE, count, tile_rows, tile_cols).transpose(2, 3, 0, 4, 1)
    back = back.reshape(count, rows, cols)
    return jnp.stack([back, jnp.zeros_like(back)], axis=1)


def norm_scale(drift, denominator):
    total = lax.psum(jnp.sum(drift * drift), ("gx", "gy"))
    return step_length / jnp.sqrt(total / denominator + epsilon)


def per_device(particles, background, obs_tile, obs_mask, obs_value, obs_var):
    count = particles.shape[0]
    tiles = particles.shape[2] // TILE * (particles.shape[3] // TILE)
    table = (obs_tile[0][:, None] == jnp.arange(tiles, dtype=jnp.int32)[None, :]).astype(
        jnp.float32
    )
    weights = obs_mask[:, 0, :].astype(jnp.float32)
    values = obs_value[0]
    variance = obs_var[0]
    local_size = particles[0].size
    total_size = float(local_size * lax.axis_size("gx") * lax.axis_size("gy"))
    pair_count = float(count * (count - 1))
    off_diag = 1.0 - jnp.eye(count, dtype=jnp.float32)
    state = particles
    gram = None
    for step in range(STEPS):
        deviation = state - background[None]
        flat_dev = deviation.reshape(count, -1)
        if gram is None:
            gram = lax.psum(jnp.dot(flat_dev, flat_dev.T, precision=highest), ("gx", "gy"))
        gradient = prior_term(deviation) + observe_term(state, table, weights, values, variance)
        flat_grad = gradient.reshape(count, -1)
        diagonal = jnp.diagonal(gram)
        distance = diagonal[:, None] + diagonal[None, :] - 2.0 * gram
        width = jnp.sum(distance * off_diag) / (pair_count * total_size) + epsilon
        kernel = jnp.exp(-distance / (2.0 * width * total_size))
        attract = jnp.dot(kernel, flat_grad, precision=highest)
        pulled = jnp.dot(kernel, flat_dev, precision=highest)
        drift = (attract + (jnp.sum(kernel, axis=1)[:, None] * flat_dev - pulled) / width) / count
        if step + 1 < STEPS:
            cross, square = lax.psum(
                (
                    jnp.dot(flat_dev, drift.T, precision=highest),
                    jnp.dot(drift, drift.T, precision=highest),
                ),
                ("gx", "gy"),
            )
            scale = step_length / jnp.sqrt(jnp.trace(square) / (count * total_size) + epsilon)
            gram = gram + scale * (cross + cross.T) + scale * scale * square
        else:
            scale = norm_scale(drift, count * total_size)
        state = state + scale * drift.reshape(state.shape)
    return state


def solution(mesh):
    return jax.shard_map(
        per_device,
        mesh=mesh,
        in_specs=(
            P(None, None, "gx", "gy"),
            P(None, "gx", "gy"),
            P("gx", "gy"),
            P(None, "gx", "gy"),
            P("gx", "gy"),
            P("gx", "gy"),
        ),
        out_specs=P(None, None, "gx", "gy"),
        check_vma=False,
    )
```

profile of v0, /device:TPU:14, one launch (start us, length us, event | category | flops | bytes accessed | tf_op | source)
XLA Modules:
  0.0 223.9 jit_solution(16743643375088304163)
XLA Ops:
  0.0 2.8 %copy.40 = f32[64,2,4,512]{0,3,2,1:T(8,128)} copy(f32[64,2,4,512]{3,2,1,0:T(4,128)} %param.6) | data formatting | bytes 2097152 | tf_op args[0]
  2.8 2.2 broadcast_subtract_fusion.1
  6.1 2.4 %copy.32 = f32[64,2,2,512]{3,0,2,1:T(8,128)} copy(f32[64,2,2,512]{0,3,2,1:T(8,128)} %get-tuple-element.15) | data formatting | bytes 1048576 | tf_op jit(solution)/shard_map/slice | solution.py:23
  13.2 3.6 %convolution_bitcast_fusion.1 = f32[64,64]{1,0:T(8,128)S(1)} fusion(f32[64,2,4,512]{0,3,2,1:T(8,128)S(1)} %broadcast_subtract_fusion.1), kind=kOutput, calls=%fused_computation.61 | convolution fusion | flops 201326592 | bytes 1064960 | tf_op jit(solution)/shard_map/dot_general | solution.py:82
  19.3 41.9 %psum.28 = f32[64,64]{1,0:T(8,128)S(1)} all-reduce(f32[64,64]{1,0:T(8,128)S(1)} %convolution_bitcast_fusion.1), channel_id=1, replica_groups=mesh['gx'=16,'gy'=2] {'gx','gy'}, use_global_device_ids=true, to_apply=%region_0.0 | all-reduce | flops 4096 | bytes 32768 | tf_op jit(solution)/shard_map/psum | solution.py:82
  65.7 3.4 %fusion.1 = f32[64,4096]{1,0:T(8,128)} fusion(f32[64,4096]{0,1:T(8,128)S(1)} %bitcast.63, f32[64,4096]{1,0:T(8,128)S(1)} %copy.57, f32[]{:T(128)S(6)} %add.128, f32[64]{0:T(128)S(1)} %fusion.55, f32[64,64]{1,0:T(8,128)S(1)} %psum.28, f32[]{:T(128)S(6)} %mul.175, f32[64]{0:T(128)S(1)} %gather_fusion), kind=kOutput, calls=%fused_computation.6 | convolution fusion | flops 202133504 | bytes 3162632 | tf_op jit(solution)/shard_map/dot_general | solution.py:90
  70.5 2.4 %copy.35 = f32[64,2,2,512]{0,3,2,1:T(8,128)} copy(f32[64,2,2,512]{3,0,2,1:T(8,128)} %collective-permute-done.1) | data formatting | bytes 1048576 | tf_op jit(solution)/shard_map/ppermute | solution.py:25
  73.8 1.9 collective-permute-start.3
  77.0 2.4 %copy.38 = f32[4,4,64,1,128]{2,1,4,0,3:T(4,128)} copy(f32[4,4,64,1,128]{4,2,1,0,3:T(8,128)} %bitcast.78) | data formatting | bytes 1048576 | tf_op jit(solution)/shard_map/reshape | solution.py:53
  81.1 2.2 %fusion.8 = f32[64,2,6,514]{0,3,2,1:T(8,128)S(1)} fusion(f32[64,2,8,516]{0,3,2,1:T(8,128)S(1)} %pad_maximum_fusion, f32[64,2,8,2]{0,3,2,1:T(2,128)S(1)} %collective-permute-done.2, f32[64,2,2,512]{0,3,2,1:T(8,128)S(1)} %copy-done.1, f32[64,2,4,512]{0,3,2,1:T(8,128)S(1)} %broadcast_subtract_fusion.1, f32[64,2,2,512]{0,3,2,1:T(8,128)S(1)} %copy.34, ...), kind=kLoop, calls=%fused_computation.25 | loop fusion | flops 5131776 | bytes 8429568 | tf_op jit(solution)/shard_map/sub | solution.py:38
  84.6 2.4 %convolution_add_fusion.1 = f32[64,4096]{1,0:T(8,128)S(1)} fusion(f32[64,4096]{1,0:T(8,128)S(1)} %copy-done.3, f32[64,4096]{0,1:T(8,128)S(1)} %bitcast.67, f32[64,64]{1,0:T(8,128)S(1)} %psum.28, f32[]{:T(128)S(6)} %mul.175, f32[64]{0:T(128)S(1)} %gather_fusion), kind=kOutput, calls=%fused_computation.7 | convolution fusion | flops 201609216 | bytes 3162372 | tf_op jit(solution)/shard_map/dot_general | solution.py:89
  89.6 39.4 %all-reduce.2 = (f32[64,64]{1,0:T(8,128)S(1)}, f32[64,64]{0,1:T(8,128)S(1)}) all-reduce(f32[64,64]{1,0:T(8,128)S(1)} %fusion.29, f32[64,64]{0,1:T(8,128)S(1)} %fusion.27), channel_id=1, replica_groups=mesh['gx'=16,'gy'=2] {'gx','gy'}, use_global_device_ids=true, to_apply=%region_4.5 | all-reduce | flops 8192 | bytes 65536 | tf_op jit(solution)/shard_map/psum | solution.py:93
  130.4 1.9 copy.58
  132.3 3.5 %broadcast_subtract_fusion = (f32[64,2,4,512]{0,3,2,1:T(8,128)S(1)}, f32[64,2,4,512]{0,3,2,1:T(8,128)}) fusion(f32[2,4,512]{2,1,0:T(4,128)S(1)} %copy-done.7, f32[64,2,4,512]{0,3,2,1:T(8,128)} %copy.40, f32[64,2,4,512]{0,3,2,1:T(8,128)} %bitcast.70), kind=kLoop, calls=%fused_computation.63 | loop fusion | flops 524288 | bytes 4210688 | tf_op jit(solution)/shard_map/sub | solution.py:79
  136.9 2.4 %copy.44 = f32[64,2,2,512]{3,0,2,1:T(8,128)} copy(f32[64,2,2,512]{0,3,2,1:T(8,128)} %get-tuple-element.13) | data formatting | bytes 1048576 | tf_op jit(solution)/shard_map/slice | solution.py:23
  149.1 3.4 %fusion = f32[64,4096]{1,0:T(8,128)} fusion(f32[64,4096]{0,1:T(8,128)S(1)} %bitcast.66, f32[64,4096]{1,0:T(8,128)S(1)} %copy.59, f32[]{:T(128)S(6)} %add.146, f32[64]{0:T(128)S(1)} %fusion.56, f32[64,64]{1,0:T(8,128)S(1)} %fusion.48, f32[]{:T(128)S(6)} %mul.204, f32[64]{0:T(128)S(1)} %gather_fusion.1), kind=kOutput, calls=%fused_computation.3 | convolution fusion | flops 202133504 | bytes 3162632 | tf_op jit(solution)/shard_map/dot_general | solution.py:90
  155.2 2.4 %copy.47 = f32[64,2,2,512]{0,3,2,1:T(8,128)} copy(f32[64,2,2,512]{3,0,2,1:T(8,128)} %collective-permute-done.5) | data formatting | bytes 1048576 | tf_op jit(solution)/shard_map/ppermute | solution.py:25
  161.6 2.4 %copy.49 = f32[4,4,64,1,128]{2,1,4,0,3:T(4,128)} copy(f32[4,4,64,1,128]{4,2,1,0,3:T(8,128)} %bitcast.77) | data formatting | bytes 1048576 | tf_op jit(solution)/shard_map/reshape | solution.py:53
  165.8 2.2 %fusion.4 = f32[64,2,6,514]{0,3,2,1:T(8,128)S(1)} fusion(f32[64,2,8,516]{0,3,2,1:T(8,128)S(1)} %pad_maximum_fusion.1, f32[64,2,8,2]{0,3,2,1:T(2,128)S(1)} %collective-permute-done.6, f32[64,2,2,512]{0,3,2,1:T(8,128)S(1)} %copy-done, f32[64,2,4,512]{0,3,2,1:T(8,128)S(1)} %get-tuple-element.7, f32[64,2,2,512]{0,3,2,1:T(8,128)S(1)} %copy.46, ...), kind=kLoop, calls=%fused_computation.13 | loop fusion | flops 5131776 | bytes 8429568 | tf_op jit(solution)/shard_map/sub | solution.py:38
  169.3 3.1 %multiply_reduce_fusion = (f32[]{:T(128)}, f32[64,4096]{1,0:T(8,128)S(1)}) fusion(f32[64,4096]{1,0:T(8,128)S(1)} %copy-done.4, f32[64,4096]{0,1:T(8,128)S(1)} %bitcast.69, f32[64,64]{1,0:T(8,128)S(1)} %fusion.48, f32[]{:T(128)S(6)} %mul.204, f32[64]{0:T(128)S(1)} %gather_fusion.1), kind=kOutput, calls=%fused_computation.62 | convolution fusion | flops 202395648 | bytes 3162376 | tf_op jit(solution)/shard_map/dot_general | solution.py:89
  172.3 43.0 %psum.31 = f32[]{:T(128)} all-reduce(f32[]{:T(128)} %get-tuple-element.17), channel_id=1, replica_groups=mesh['gx'=16,'gy'=2] {'gx','gy'}, use_global_device_ids=true, to_apply=%region_11.12 | all-reduce | flops 1 | bytes 8 | tf_op jit(solution)/shard_map/psum | solution.py:59
  216.2 1.9 copy.60
  218.1 3.2 %add.157 = f32[64,2,4,512]{0,3,2,1:T(8,128)} add(f32[64,2,4,512]{0,3,2,1:T(8,128)S(1)} %copy-done.2, f32[64,2,4,512]{0,3,2,1:T(8,128)} %bitcast.68) | non-fusion elementwise | flops 262144 | bytes 3145728 | tf_op jit(solution)/shard_map/add | solution.py:104
  221.2 2.7 %copy.52 = f32[64,2,4,512]{3,2,1,0:T(4,128)} copy(f32[64,2,4,512]{0,3,2,1:T(8,128)} %add.157) | data formatting | bytes 2097152 | tf_op jit(solution)/shard_map/add | solution.py:104
  (80 shorter events, 41.9 us)
Async XLA Ops:
  0.0 2.8 %copy-start.7 = (f32[2,4,512]{2,1,0:T(4,128)S(1)}, f32[2,4,512]{2,1,0:T(4,128)}, u32[]{:S(2)}) copy-start(f32[2,4,512]{2,1,0:T(4,128)} %param.7) | copy-start | bytes 49156
  8.5 60.7 %collective-permute-start = (f32[64,2,2,512]{3,0,2,1:T(8,128)}, f32[64,2,2,512]{3,0,2,1:T(8,128)}, u32[]{:S(2)}, u32[]{:S(2)}) collective-permute-start(f32[64,2,2,512]{3,0,2,1:T(8,128)} %copy.32), channel_id=1, source_target_pairs={{0,2},{2,4},{4,6},{6,8},{8,10},{10,12},{12,14},{14,16},{16,18},{18... | collective-permute-start | bytes 1572872 | tf_op jit(solution)/shard_map/ppermute | solution.py:22
  9.6 60.9 %collective-permute-start.1 = (f32[64,2,2,512]{3,0,2,1:T(8,128)}, f32[64,2,2,512]{3,0,2,1:T(8,128)}, u32[]{:S(2)}, u32[]{:S(2)}) collective-permute-start(f32[64,2,2,512]{3,0,2,1:T(8,128)} %copy.33), channel_id=1, source_target_pairs={{2,0},{4,2},{6,4},{8,6},{10,8},{12,10},{14,12},{16,14},{18,16},{20... | collective-permute-start | bytes 1572872 | tf_op jit(solution)/shard_map/ppermute | solution.py:25
  13.2 3.6 %copy-start.8 = (s32[16,1,128]{2,1,0:T(1,128)S(1)}, s32[16,1,128]{2,1,0:T(1,128)}, u32[]{:S(2)}) copy-start(s32[16,1,128]{2,1,0:T(1,128)} %param.9) | copy-start | bytes 24580
  19.3 44.8 %copy-start.9 = (s32[1,128]{1,0:T(1,128)S(1)}, s32[1,128]{1,0:T(1,128)}, u32[]{:S(2)}) copy-start(s32[1,128]{1,0:T(1,128)} %param.8) | copy-start | bytes 1540
  61.2 4.5 %copy-start.10 = (f32[1,128]{1,0:T(1,128)S(1)}, f32[1,128]{1,0:T(1,128)}, u32[]{:S(2)}) copy-start(f32[1,128]{1,0:T(1,128)} %param.11) | copy-start | bytes 1540
  61.2 4.4 %copy-start.11 = (f32[1,128]{1,0:T(1,128)S(1)}, f32[1,128]{1,0:T(1,128)}, u32[]{:S(2)}) copy-start(f32[1,128]{1,0:T(1,128)} %param.10) | copy-start | bytes 1540
  73.7 5.7 %collective-permute-start.2 = (f32[64,2,8,2]{0,3,2,1:T(2,128)S(1)}, f32[64,2,8,2]{0,3,2,1:T(2,128)S(1)}, u32[]{:S(2)}, u32[]{:S(2)}) collective-permute-start(f32[64,2,8,2]{0,3,2,1:T(2,128)S(1)} %get-tuple-element.11), channel_id=1, source_target_pairs={{0,1},{1,0},{2,3},{3,2},{4,5},{5,4},{6,7},{7,6},{8,9},{9,8},{10,11... | collective-permute-start | bytes 24584 | tf_op jit(solution)/shard_map/ppermute | solution.py:22
  73.8 5.5 %collective-permute-start.3 = (f32[64,2,8,2]{0,3,2,1:T(2,128)S(1)}, f32[64,2,8,2]{0,3,2,1:T(2,128)S(1)}, u32[]{:S(2)}, u32[]{:S(2)}) collective-permute-start(f32[64,2,8,2]{0,3,2,1:T(2,128)S(1)} %get-tuple-element.12), channel_id=1, source_target_pairs={{1,0},{0,1},{3,2},{2,3},{5,4},{4,5},{7,6},{6,7},{9,8},{8,9},{11,10... | collective-permute-start | bytes 24584 | tf_op jit(solution)/shard_map/ppermute | solution.py:25
  79.3 1.8 copy-start.1
  81.1 2.3 %copy-start.6 = (f32[4,4,64,1,128]{2,1,4,0,3:T(4,128)S(1)}, f32[4,4,64,1,128]{2,1,4,0,3:T(4,128)}, u32[]{:S(2)}) copy-start(f32[4,4,64,1,128]{2,1,4,0,3:T(4,128)} %copy.38) | copy-start | bytes 1572868
  83.4 1.2 copy-start.3
  139.3 14.5 %collective-permute-start.4 = (f32[64,2,2,512]{3,0,2,1:T(8,128)}, f32[64,2,2,512]{3,0,2,1:T(8,128)}, u32[]{:S(2)}, u32[]{:S(2)}) collective-permute-start(f32[64,2,2,512]{3,0,2,1:T(8,128)} %copy.44), channel_id=1, source_target_pairs={{0,2},{2,4},{4,6},{6,8},{8,10},{10,12},{12,14},{14,16},{16,18},{18... | collective-permute-start | bytes 1572872 | tf_op jit(solution)/shard_map/ppermute | solution.py:22
  140.4 14.8 %collective-permute-start.5 = (f32[64,2,2,512]{3,0,2,1:T(8,128)}, f32[64,2,2,512]{3,0,2,1:T(8,128)}, u32[]{:S(2)}, u32[]{:S(2)}) collective-permute-start(f32[64,2,2,512]{3,0,2,1:T(8,128)} %copy.45), channel_id=1, source_target_pairs={{2,0},{4,2},{6,4},{8,6},{10,8},{12,10},{14,12},{16,14},{18,16},{20... | collective-permute-start | bytes 1572872 | tf_op jit(solution)/shard_map/ppermute | solution.py:25
  158.3 5.7 %collective-permute-start.6 = (f32[64,2,8,2]{0,3,2,1:T(2,128)S(1)}, f32[64,2,8,2]{0,3,2,1:T(2,128)S(1)}, u32[]{:S(2)}, u32[]{:S(2)}) collective-permute-start(f32[64,2,8,2]{0,3,2,1:T(2,128)S(1)} %get-tuple-element.9), channel_id=1, source_target_pairs={{0,1},{1,0},{2,3},{3,2},{4,5},{5,4},{6,7},{7,6},{8,9},{9,8},{10,11... | collective-permute-start | bytes 24584 | tf_op jit(solution)/shard_map/ppermute | solution.py:22
  159.6 4.4 %collective-permute-start.7 = (f32[64,2,8,2]{0,3,2,1:T(2,128)S(1)}, f32[64,2,8,2]{0,3,2,1:T(2,128)S(1)}, u32[]{:S(2)}, u32[]{:S(2)}) collective-permute-start(f32[64,2,8,2]{0,3,2,1:T(2,128)S(1)} %get-tuple-element.10), channel_id=1, source_target_pairs={{1,0},{0,1},{3,2},{2,3},{5,4},{4,5},{7,6},{6,7},{9,8},{8,9},{11,10... | collective-permute-start | bytes 24584 | tf_op jit(solution)/shard_map/ppermute | solution.py:25
  164.0 1.8 copy-start
  165.8 2.3 %copy-start.5 = (f32[4,4,64,1,128]{2,1,4,0,3:T(4,128)S(1)}, f32[4,4,64,1,128]{2,1,4,0,3:T(4,128)}, u32[]{:S(2)}) copy-start(f32[4,4,64,1,128]{2,1,4,0,3:T(4,128)} %copy.49) | copy-start | bytes 1572868
  168.0 1.2 copy-start.4
  216.1 1.9 copy-start.2
where the time goes:
time: 225 us; the launch traced here: 224 us
  blocking collectives  124 us (55%)
  local copies, waits for them, and re-layouts  40.5 us (18%)
  matrix products  23.9 us (11%)
  other arithmetic  23.2 us (10%)
  starting transfers between devices  7.67 us (3%)
  between operations  3.05 us (1%)
    psum x1, blocking collectives, norm_scale(): total = lax.psum(jnp.sum(drift * drift), ('gx', 'gy'))  43 us
    psum x1, blocking collectives, per_device(): lax.psum(jnp.dot(flat_dev, flat_dev.T, precision=highest), ('gx', 'gy'))  41.9 us
    psum x1, blocking collectives, per_device(): lax.psum((jnp.dot(flat_dev, drift.T, precision=highest), jnp.dot(drift, d...  39.4 us
    slice x4, local copies, waits for them, and re-layouts, with_halo(): lax.slice_in_dim(block, block.shape[dim] - width, None, axis=dim)  6.94 us
    dot_general x2, matrix products, per_device(): pulled = jnp.dot(kernel, flat_dev, precision=highest)  6.85 us
    ppermute x4, starting transfers between devices, with_halo(): lax.ppermute(lax.slice_in_dim(block, 0, width, axis=dim), axis, backward)  6.21 us
    sub x2, other arithmetic, per_device(): deviation = state - background[None]  5.68 us
    dot_general x2, matrix products, per_device(): attract = jnp.dot(kernel, flat_grad, precision=highest)  5.5 us
  transfers between devices with their start and end apart: 8, of which 1 were waited for; matrix products, arithmetic and copies ran while one was open for 17% of the time, Pallas kernels for 0%

commit v1 on v0

--- a/solution.py
+++ b/solution.py
@@ -91,11 +91,14 @@
         drift = (attract + (jnp.sum(kernel, axis=1)[:, None] * flat_dev - pulled) / width) / count
         if step + 1 < STEPS:
             cross, square = lax.psum(
-                (
-                    jnp.dot(flat_dev, drift.T, precision=highest),
-                    jnp.dot(drift, drift.T, precision=highest),
+                lax.psum(
+                    (
+                        jnp.dot(flat_dev, drift.T, precision=highest),
+                        jnp.dot(drift, drift.T, precision=highest),
+                    ),
+                    "gy",
                 ),
-                ("gx", "gy"),
+                "gx",
             )
             scale = step_length / jnp.sqrt(jnp.trace(square) / (count * total_size) + epsilon)
             gram = gram + scale * (cross + cross.T) + scale * scale * square

time: 225 us -> 250 us (1.11)
  blocking collectives: 124 us -> 148 us
    psum x0 -> x1, blocking collectives: none -> 45 us  [per_device(): lax.psum(lax.psum((jnp.dot(flat_dev, drift.T, precision=highest), jnp.dot...]
    psum x1, blocking collectives: 39.4 us -> 7.58 us  [per_device(): lax.psum((jnp.dot(flat_dev, drift.T, precision=highest), jnp.dot(drift, d...]
    psum x1, blocking collectives: 43 us -> 53.2 us  [norm_scale(): total = lax.psum(jnp.sum(drift * drift), ('gx', 'gy'))]
  transfers between devices with their start and end apart: 8 -> 8, of which waited for: 1 -> 1; matrix products, arithmetic and copies ran while one was open for 17% -> 15% of each run, Pallas kernels for 0% -> 0%
where the time goes in v1:
time: 250 us; the launch traced here: 247 us
  blocking collectives  148 us (59%)
  local copies, waits for them, and re-layouts  40.5 us (16%)
  matrix products  23.9 us (10%)
  other arithmetic  23.2 us (9%)
  starting transfers between devices  7.67 us (3%)
  between operations  3.05 us (1%)
    psum x1, blocking collectives, norm_scale(): total = lax.psum(jnp.sum(drift * drift), ('gx', 'gy'))  53.2 us
    psum x1, blocking collectives, per_device(): lax.psum(lax.psum((jnp.dot(flat_dev, drift.T, precision=highest), jnp.dot...  45 us
    psum x1, blocking collectives, per_device(): lax.psum(jnp.dot(flat_dev, flat_dev.T, precision=highest), ('gx', 'gy'))  41.9 us
    psum x1, blocking collectives, per_device(): lax.psum((jnp.dot(flat_dev, drift.T, precision=highest), jnp.dot(drift, d...  7.58 us
    slice x4, local copies, waits for them, and re-layouts, with_halo(): lax.slice_in_dim(block, block.shape[dim] - width, None, axis=dim)  6.92 us
    dot_general x2, matrix products, per_device(): pulled = jnp.dot(kernel, flat_dev, precision=highest)  6.85 us
    ppermute x4, starting transfers between devices, with_halo(): lax.ppermute(lax.slice_in_dim(block, 0, width, axis=dim), axis, backward)  5.78 us
    sub x2, other arithmetic, per_device(): deviation = state - background[None]  5.68 us
  transfers between devices with their start and end apart: 8, of which 1 were waited for; matrix products, arithmetic and copies ran while one was open for 15% of the time, Pallas kernels for 0%

profile of v1, /device:TPU:14, one launch (start us, length us, event | category | flops | bytes accessed | tf_op | source)
XLA Modules:
  0.0 247.2 jit_solution(18200161593746304538)
XLA Ops:
  0.0 2.8 %copy.40 = f32[64,2,4,512]{0,3,2,1:T(8,128)} copy(f32[64,2,4,512]{3,2,1,0:T(4,128)} %param.6) | data formatting | bytes 2097152 | tf_op args[0]
  2.8 2.2 broadcast_subtract_fusion.1
  6.1 2.4 copy.32
  13.2 3.6 %convolution_bitcast_fusion.1 = f32[64,64]{1,0:T(8,128)S(1)} fusion(f32[64,2,4,512]{0,3,2,1:T(8,128)S(1)} %broadcast_subtract_fusion.1), kind=kOutput, calls=%fused_computation.61 | convolution fusion | flops 201326592 | bytes 1064960 | tf_op jit(solution)/shard_map/dot_general | solution.py:82
  19.3 41.9 %psum.42 = f32[64,64]{1,0:T(8,128)S(1)} all-reduce(f32[64,64]{1,0:T(8,128)S(1)} %convolution_bitcast_fusion.1), channel_id=1, replica_groups=mesh['gx'=16,'gy'=2] {'gx','gy'}, use_global_device_ids=true, to_apply=%region_0.0 | all-reduce | flops 4096 | bytes 32768 | tf_op jit(solution)/shard_map/psum | solution.py:82
  65.7 3.4 %fusion.1 = f32[64,4096]{1,0:T(8,128)} fusion(f32[64,4096]{0,1:T(8,128)S(1)} %bitcast.63, f32[64,4096]{1,0:T(8,128)S(1)} %copy.57, f32[]{:T(128)S(6)} %add.132, f32[64]{0:T(128)S(1)} %fusion.55, f32[64,64]{1,0:T(8,128)S(1)} %psum.42, f32[]{:T(128)S(6)} %mul.175, f32[64]{0:T(128)S(1)} %gather_fusion), kind=kOutput, calls=%fused_computation.6 | convolution fusion | flops 202133504 | bytes 3162632 | tf_op jit(solution)/shard_map/dot_general | solution.py:90
  70.5 2.4 copy.35
  73.8 2.0 collective-permute-start.3
  77.0 2.4 copy.38
  81.1 2.2 fusion.8
  84.6 2.4 convolution_add_fusion.1
  89.6 7.6 %all-reduce.3 = (f32[64,64]{1,0:T(8,128)S(1)}, f32[64,64]{0,1:T(8,128)S(1)}) all-reduce(f32[64,64]{1,0:T(8,128)S(1)} %fusion.29, f32[64,64]{0,1:T(8,128)S(1)} %fusion.27), channel_id=1, replica_groups=mesh['gx'=16,'gy'=2] {'gy'}, use_global_device_ids=true, to_apply=%region_4.5 | all-reduce | flops 8192 | bytes 65536 | tf_op jit(solution)/shard_map/psum | solution.py:94
  97.2 45.0 %all-reduce.2 = (f32[64,64]{1,0:T(8,128)S(1)}, f32[64,64]{0,1:T(8,128)S(1)}) all-reduce(f32[64,64]{1,0:T(8,128)S(1)} %get-tuple-element.7, f32[64,64]{0,1:T(8,128)S(1)} %get-tuple-element.8), channel_id=1, replica_groups=mesh['gx'=16,'gy'=2] {'gx'}, use_global_device_ids=true, to_apply=%region_5.6 | all-reduce | flops 8192 | bytes 65536 | tf_op jit(solution)/shard_map/psum | solution.py:93
  143.5 1.9 copy.58
  145.4 3.5 %broadcast_subtract_fusion = (f32[64,2,4,512]{0,3,2,1:T(8,128)S(1)}, f32[64,2,4,512]{0,3,2,1:T(8,128)}) fusion(f32[2,4,512]{2,1,0:T(4,128)S(1)} %copy-done.7, f32[64,2,4,512]{0,3,2,1:T(8,128)} %copy.40, f32[64,2,4,512]{0,3,2,1:T(8,128)} %bitcast.70), kind=kLoop, calls=%fused_computation.63 | loop fusion | flops 524288 | bytes 4210688 | tf_op jit(solution)/shard_map/sub | solution.py:79
  150.0 2.4 copy.44
  162.2 3.4 %fusion = f32[64,4096]{1,0:T(8,128)} fusion(f32[64,4096]{0,1:T(8,128)S(1)} %bitcast.66, f32[64,4096]{1,0:T(8,128)S(1)} %copy.59, f32[]{:T(128)S(6)} %add.150, f32[64]{0:T(128)S(1)} %fusion.56, f32[64,64]{1,0:T(8,128)S(1)} %fusion.48, f32[]{:T(128)S(6)} %mul.204, f32[64]{0:T(128)S(1)} %gather_fusion.1), kind=kOutput, calls=%fused_computation.3 | convolution fusion | flops 202133504 | bytes 3162632 | tf_op jit(solution)/shard_map/dot_general | solution.py:90
  168.3 2.4 copy.47
  174.8 2.4 copy.49
  178.9 2.2 fusion.4
  182.4 3.1 %multiply_reduce_fusion = (f32[]{:T(128)}, f32[64,4096]{1,0:T(8,128)S(1)}) fusion(f32[64,4096]{1,0:T(8,128)S(1)} %copy-done.4, f32[64,4096]{0,1:T(8,128)S(1)} %bitcast.69, f32[64,64]{1,0:T(8,128)S(1)} %fusion.48, f32[]{:T(128)S(6)} %mul.204, f32[64]{0:T(128)S(1)} %gather_fusion.1), kind=kOutput, calls=%fused_computation.62 | convolution fusion | flops 202395648 | bytes 3162376 | tf_op jit(solution)/shard_map/dot_general | solution.py:89
  185.5 53.2 %psum.47 = f32[]{:T(128)} all-reduce(f32[]{:T(128)} %get-tuple-element.19), channel_id=1, replica_groups=mesh['gx'=16,'gy'=2] {'gx','gy'}, use_global_device_ids=true, to_apply=%region_13.14 | all-reduce | flops 1 | bytes 8 | tf_op jit(solution)/shard_map/psum | solution.py:59
  241.3 3.2 %add.161 = f32[64,2,4,512]{0,3,2,1:T(8,128)} add(f32[64,2,4,512]{0,3,2,1:T(8,128)S(1)} %copy-done.2, f32[64,2,4,512]{0,3,2,1:T(8,128)} %bitcast.68) | non-fusion elementwise | flops 262144 | bytes 3145728 | tf_op jit(solution)/shard_map/add | solution.py:107
  244.5 2.7 %copy.52 = f32[64,2,4,512]{3,2,1,0:T(4,128)} copy(f32[64,2,4,512]{0,3,2,1:T(8,128)} %add.161) | data formatting | bytes 2097152 | tf_op jit(solution)/shard_map/add | solution.py:107
  (81 shorter events, 43.8 us)
Async XLA Ops:
  0.0 2.8 %copy-start.7 = (f32[2,4,512]{2,1,0:T(4,128)S(1)}, f32[2,4,512]{2,1,0:T(4,128)}, u32[]{:S(2)}) copy-start(f32[2,4,512]{2,1,0:T(4,128)} %param.7) | copy-start | bytes 49156
  8.5 60.7 %collective-permute-start = (f32[64,2,2,512]{3,0,2,1:T(8,128)}, f32[64,2,2,512]{3,0,2,1:T(8,128)}, u32[]{:S(2)}, u32[]{:S(2)}) collective-permute-start(f32[64,2,2,512]{3,0,2,1:T(8,128)} %copy.32), channel_id=1, source_target_pairs={{0,2},{2,4},{4,6},{6,8},{8,10},{10,12},{12,14},{14,16},{16,18},{18... | collective-permute-start | bytes 1572872 | tf_op jit(solution)/shard_map/ppermute | solution.py:22
  9.6 60.9 %collective-permute-start.1 = (f32[64,2,2,512]{3,0,2,1:T(8,128)}, f32[64,2,2,512]{3,0,2,1:T(8,128)}, u32[]{:S(2)}, u32[]{:S(2)}) collective-permute-start(f32[64,2,2,512]{3,0,2,1:T(8,128)} %copy.33), channel_id=1, source_target_pairs={{2,0},{4,2},{6,4},{8,6},{10,8},{12,10},{14,12},{16,14},{18,16},{20... | collective-permute-start | bytes 1572872 | tf_op jit(solution)/shard_map/ppermute | solution.py:25
  13.2 3.6 %copy-start.8 = (s32[16,1,128]{2,1,0:T(1,128)S(1)}, s32[16,1,128]{2,1,0:T(1,128)}, u32[]{:S(2)}) copy-start(s32[16,1,128]{2,1,0:T(1,128)} %param.9) | copy-start | bytes 24580
  19.3 44.8 %copy-start.9 = (s32[1,128]{1,0:T(1,128)S(1)}, s32[1,128]{1,0:T(1,128)}, u32[]{:S(2)}) copy-start(s32[1,128]{1,0:T(1,128)} %param.8) | copy-start | bytes 1540
  61.2 4.5 %copy-start.10 = (f32[1,128]{1,0:T(1,128)S(1)}, f32[1,128]{1,0:T(1,128)}, u32[]{:S(2)}) copy-start(f32[1,128]{1,0:T(1,128)} %param.11) | copy-start | bytes 1540
  61.2 4.5 %copy-start.11 = (f32[1,128]{1,0:T(1,128)S(1)}, f32[1,128]{1,0:T(1,128)}, u32[]{:S(2)}) copy-start(f32[1,128]{1,0:T(1,128)} %param.10) | copy-start | bytes 1540
  73.7 5.7 %collective-permute-start.2 = (f32[64,2,8,2]{0,3,2,1:T(2,128)S(1)}, f32[64,2,8,2]{0,3,2,1:T(2,128)S(1)}, u32[]{:S(2)}, u32[]{:S(2)}) collective-permute-start(f32[64,2,8,2]{0,3,2,1:T(2,128)S(1)} %get-tuple-element.13), channel_id=1, source_target_pairs={{0,1},{1,0},{2,3},{3,2},{4,5},{5,4},{6,7},{7,6},{8,9},{9,8},{10,11... | collective-permute-start | bytes 24584 | tf_op jit(solution)/shard_map/ppermute | solution.py:22
  73.8 5.6 %collective-permute-start.3 = (f32[64,2,8,2]{0,3,2,1:T(2,128)S(1)}, f32[64,2,8,2]{0,3,2,1:T(2,128)S(1)}, u32[]{:S(2)}, u32[]{:S(2)}) collective-permute-start(f32[64,2,8,2]{0,3,2,1:T(2,128)S(1)} %get-tuple-element.14), channel_id=1, source_target_pairs={{1,0},{0,1},{3,2},{2,3},{5,4},{4,5},{7,6},{6,7},{9,8},{8,9},{11,10... | collective-permute-start | bytes 24584 | tf_op jit(solution)/shard_map/ppermute | solution.py:25
  79.3 1.8 copy-start.1
  81.1 2.3 copy-start.6
  83.4 1.2 copy-start.3
  152.4 14.5 %collective-permute-start.4 = (f32[64,2,2,512]{3,0,2,1:T(8,128)}, f32[64,2,2,512]{3,0,2,1:T(8,128)}, u32[]{:S(2)}, u32[]{:S(2)}) collective-permute-start(f32[64,2,2,512]{3,0,2,1:T(8,128)} %copy.44), channel_id=1, source_target_pairs={{0,2},{2,4},{4,6},{6,8},{8,10},{10,12},{12,14},{14,16},{16,18},{18... | collective-permute-start | bytes 1572872 | tf_op jit(solution)/shard_map/ppermute | solution.py:22
  153.5 14.8 %collective-permute-start.5 = (f32[64,2,2,512]{3,0,2,1:T(8,128)}, f32[64,2,2,512]{3,0,2,1:T(8,128)}, u32[]{:S(2)}, u32[]{:S(2)}) collective-permute-start(f32[64,2,2,512]{3,0,2,1:T(8,128)} %copy.45), channel_id=1, source_target_pairs={{2,0},{4,2},{6,4},{8,6},{10,8},{12,10},{14,12},{16,14},{18,16},{20... | collective-permute-start | bytes 1572872 | tf_op jit(solution)/shard_map/ppermute | solution.py:25
  171.4 5.7 %collective-permute-start.6 = (f32[64,2,8,2]{0,3,2,1:T(2,128)S(1)}, f32[64,2,8,2]{0,3,2,1:T(2,128)S(1)}, u32[]{:S(2)}, u32[]{:S(2)}) collective-permute-start(f32[64,2,8,2]{0,3,2,1:T(2,128)S(1)} %get-tuple-element.11), channel_id=1, source_target_pairs={{0,1},{1,0},{2,3},{3,2},{4,5},{5,4},{6,7},{7,6},{8,9},{9,8},{10,11... | collective-permute-start | bytes 24584 | tf_op jit(solution)/shard_map/ppermute | solution.py:22
  173.2 3.9 %collective-permute-start.7 = (f32[64,2,8,2]{0,3,2,1:T(2,128)S(1)}, f32[64,2,8,2]{0,3,2,1:T(2,128)S(1)}, u32[]{:S(2)}, u32[]{:S(2)}) collective-permute-start(f32[64,2,8,2]{0,3,2,1:T(2,128)S(1)} %get-tuple-element.12), channel_id=1, source_target_pairs={{1,0},{0,1},{3,2},{2,3},{5,4},{4,5},{7,6},{6,7},{9,8},{8,9},{11,10... | collective-permute-start | bytes 24584 | tf_op jit(solution)/shard_map/ppermute | solution.py:25
  177.1 1.8 copy-start
  178.9 2.3 copy-start.5
  181.2 1.2 copy-start.4
  239.4 1.9 copy-start.2
